TPU v7x, 128 devices: a whole 4x4x4 slice. The times are simulated.
128 devices in a mesh: sx: 4 (over y), ly: 32 (over z, x, core).
Axes of the slice: x: 4, y: 4, z: 4, core: 2. Of those that a mesh axis runs over, the one named last changes fastest.
Arguments:
- tensor: float32 [1024, 1280, 512], P('sx', 'ly'), may hold values from -6 to 6
- factor_y: float32 [512, 160], replicated, may hold values from -6 to 6
- factor_z: float32 [1280, 160], P('ly'), may hold values from -6 to 6
- test_matrix: float32 [1280, 160], replicated, may hold values from -6 to 6
Outputs:
- basis_first: float32 [1024, 160], P('sx')
- basis_second: float32 [160, 512, 160], P('sx', 'ly')
- last_core: float32 [160, 1280], replicated
All inputs are finite; a program needn't handle non-finite values.
Results may differ from a plain program's by a relative error of at most 0.0003.
Values sent between devices are 32-bit elements; how exact they have to be, the bound alone decides.
No kernel may reach another device: no remote copies, remote signals or barrier semaphores. Data moves between devices by JAX's collectives and lax.ppermute only.
A program may use at most 192 MiB of HBM per device.

v0:
```python
import math

import jax
import jax.numpy as jnp
from jax import lax
from jax.experimental import pallas as pl
from jax.experimental.pallas import tpu as pltpu
from jax.sharding import PartitionSpec as P

HI = lax.Precision.HIGHEST
F32 = jnp.float32
VMEM_LIMIT = 56 * 1024 * 1024


def mm(a, b):
    return lax.dot_general(a, b, (((1,), (0,)), ((), ())), precision=HI, preferred_element_type=F32)


def mm_nt(a, b):
    return lax.dot_general(a, b, (((1,), (1,)), ((), ())), precision=HI, preferred_element_type=F32)


GROUP = 5


def tiles_of(ref, size, row0=0):
    lanes = -(-size // 128)
    return [
        [ref[row0 + 8 * t : row0 + 8 * t + 8, 128 * l : 128 * l + 128] for l in range(lanes)]
        for t in range(size // 8)
    ]

def spread(row, tile):
    return jnp.broadcast_to(tile[row : row + 1, :], (8, 128))

def put_inverse(tiles, size, out_ref, group=GROUP):
    count = size // 8
    lanes = -(-size // 128)
    lane = lax.broadcasted_iota(jnp.int32, (8, 128), 1)
    sub = lax.broadcasted_iota(jnp.int32, (8, 128), 0)
    work = [list(r) for r in tiles]
    for g in range(0, count, group):
        end = min(g + group, count)
        done = []
        for p in range(g, end):
            l0, c0 = divmod(8 * p, 128)
            span = range(p, end)
            cols = {t: [jnp.broadcast_to(work[t][l0][:, c0 + i : c0 + i + 1], (8, 128)) for i in range(8)] for t in span}
            block = list(cols[p])
            unit = [jnp.where(sub == c, 1.0, 0.0) for c in range(8)]
            diag = None
            for i in range(8):
                diag = block[i] if i == 0 else jnp.where(sub == i, block[i], diag)
                if i == 7:
                    break
                factor = block[i] * spread(i, 1.0 / block[i])
                factor = jnp.where(sub > i, factor, 0.0)
                for m in range(i + 1, 8):
                    block[m] = block[m] - factor * spread(i, block[m])
                for c in range(i + 1):
                    unit[c] = unit[c] - factor * spread(i, unit[c])
            root = lax.rsqrt(diag)
            root = root * (1.5 - 0.5 * diag * root * root)
            inv = [u * root for u in unit]
            src = list(work[p])
            inside = (lane >= c0) & (lane < c0 + 8)
            src[l0] = jnp.where(inside, jnp.where(lane - c0 == sub, 1.0, 0.0), src[l0])
            rows = []
            for l in range(lanes):
                terms = [inv[i] * spread(i, src[l]) for i in range(8)]
                rows.append(((terms[0] + terms[1]) + (terms[2] + terms[3])) + ((terms[4] + terms[5]) + (terms[6] + terms[7])))
            for l in range(lanes):
                pos = lane + 128 * l
                out_ref[8 * p : 8 * p + 8, 128 * l : 128 * l + 128] = jnp.where(pos <= sub + 8 * p, rows[l], 0.0)
            done.append(rows)
            for t in range(p + 1, end):
                factors = []
                for m in range(8):
                    terms = [cols[t][i] * spread(m, inv[i]) for i in range(m + 1)]
                    while len(terms) > 1:
                        terms = [a + b for a, b in zip(terms[::2], terms[1::2])] + ([terms[-1]] if len(terms) % 2 else [])
                    factors.append(terms[0])
                for l in range(lanes):
                    old = work[t][l]
                    if l == l0:
                        old = jnp.where(inside, 0.0, old)
                    terms = [factors[m] * spread(m, rows[l]) for m in range(8)]
                    work[t][l] = old - (((terms[0] + terms[1]) + (terms[2] + terms[3])) + ((terms[4] + terms[5]) + (terms[6] + terms[7])))
        if end < count:
            left = jnp.concatenate([jnp.concatenate(r, axis=1) for r in done], axis=0)
            pos = lax.broadcasted_iota(jnp.int32, left.shape, 1)
            own = lax.broadcasted_iota(jnp.int32, left.shape, 0) + 8 * g
            right = jnp.where((pos > own) & (pos < 8 * end), 0.0, left)
            outer = lax.dot_general(left, right, (((0,), (0,)), ((), ())), precision=HI, preferred_element_type=F32)
            for t in range(end, count):
                for l in range(lanes):
                    pos = lane + 128 * l
                    old = work[t][l]
                    if 128 * l < 8 * end and 128 * l + 128 > 8 * g:
                        old = jnp.where((pos >= 8 * g) & (pos < 8 * end), 0.0, old)
                    work[t][l] = old - outer[8 * t : 8 * t + 8, 128 * l : 128 * l + 128]


def first_kernel(index_ref, sketch_ref, q_ref, basis_ref, gram_ref, inv_ref, qt_ref, *, rank, rows_x, scale):
    sk = sketch_ref[...]
    gram_ref[...] = jnp.zeros_like(gram_ref)
    gram_ref[:, :rank] = lax.dot_general(
        sk, sk, (((0,), (0,)), ((), ())), precision=HI, preferred_element_type=F32
    )
    put_inverse(tiles_of(gram_ref, rank), rank, inv_ref)
    qt = mm_nt(inv_ref[:, :rank], sk)
    qt_ref[...] = qt
    gram_ref[:, :rank] = mm_nt(qt, qt)
    put_inverse(tiles_of(gram_ref, rank), rank, inv_ref)
    at = pl.multiple_of(index_ref[0] * rows_x, 128)
    mine = mm(inv_ref[:, :rank], qt_ref[:, pl.ds(at, rows_x)])
    q_ref[...] = mine
    basis_ref[...] = scale * mine


def first_basis(sketch, index, rows_x, scale):
    total, rank = sketch.shape
    wide = -(-rank // 128) * 128
    shape = jax.ShapeDtypeStruct((rank, rows_x), F32)
    import functools

    vmem = pl.BlockSpec(memory_space=pltpu.VMEM)
    return pl.pallas_call(
        functools.partial(first_kernel, rank=rank, rows_x=rows_x, scale=scale),
        out_shape=(shape, shape),
        in_specs=[pl.BlockSpec(memory_space=pltpu.SMEM), vmem],
        out_specs=(vmem, vmem),
        scratch_shapes=[
            pltpu.VMEM((rank, wide), F32),
            pltpu.VMEM((rank, wide), F32),
            pltpu.VMEM((rank, total), F32),
        ],
        compiler_params=pltpu.CompilerParams(vmem_limit_bytes=VMEM_LIMIT),
        name="first_basis",
    )(index, sketch)


def split(value):
    high = value.astype(jnp.bfloat16)
    rest = value - high.astype(F32)
    middle = rest.astype(jnp.bfloat16)
    low = (rest - middle.astype(F32)).astype(jnp.bfloat16)
    return high, middle, low


def dot_bf16(a, b):
    return lax.dot_general(a, b, (((1,), (0,)), ((), ())), preferred_element_type=F32)


def product_kernel(qt_ref, slab_ref, out_ref, left_ref, *, cols_z, rows_x, parts, rank_part):
    rank = parts * rank_part

    @pl.when(pl.program_id(0) == 0)
    def _():
        for n, piece in enumerate(split(qt_ref[...])):
            left_ref[n * rank : (n + 1) * rank, :] = piece

    def body(step, carry):
        z = step * 2
        left = slab_ref[pl.ds(z, rows_x, stride=cols_z), :]
        right = slab_ref[pl.ds(z + 1, rows_x, stride=cols_z), :]
        high, middle, low = split(jnp.concatenate([left, right], axis=1))
        first = dot_bf16(left_ref[...], high)
        second = dot_bf16(left_ref[: 2 * rank, :], middle)
        third = dot_bf16(left_ref[:rank, :], low)
        both = first[:rank] + (
            (first[rank : 2 * rank] + second[:rank]) + (first[2 * rank :] + (second[rank:] + third))
        )
        for s in range(parts):
            piece = both[s * rank_part : (s + 1) * rank_part]
            out_ref[s, 0, pl.ds(z, rank_part, stride=cols_z), :] = piece[:, :128]
            out_ref[s, 0, pl.ds(z + 1, rank_part, stride=cols_z), :] = piece[:, 128:]
        return carry

    lax.fori_loop(0, cols_z // 2, body, 0, unroll=10)


def product(qt, tensor, parts):
    import functools

    rows_x, cols_z, cols_y = tensor.shape
    rank = qt.shape[0]
    blocks = cols_y // 128
    rank_part = rank // parts
    flat = tensor.reshape(rows_x * cols_z, cols_y)
    return pl.pallas_call(
        functools.partial(
            product_kernel, cols_z=cols_z, rows_x=rows_x, parts=parts, rank_part=rank_part
        ),
        grid=(blocks,),
        out_shape=jax.ShapeDtypeStruct((parts, blocks, rank_part * cols_z, 128), F32),
        in_specs=[
            pl.BlockSpec((rank, rows_x), lambda i: (0, 0)),
            pl.BlockSpec((rows_x * cols_z, 128), lambda i: (0, i)),
        ],
        out_specs=pl.BlockSpec((parts, 1, rank_part * cols_z, 128), lambda i: (0, i, 0, 0)),
        scratch_shapes=[pltpu.VMEM((3 * rank, rows_x), jnp.bfloat16)],
        compiler_params=pltpu.CompilerParams(vmem_limit_bytes=VMEM_LIMIT),
        name="product",
    )(qt, flat)


def second_kernel(recv_ref, test_ref, core_ref, second_ref, gram_out_ref, gram_ref, *, width):
    step = pl.program_id(0)
    core = recv_ref[0, :, 0] + recv_ref[1, :, 0]
    core = core + (recv_ref[2, :, 0] + recv_ref[3, :, 0])
    core = core.reshape(core_ref.shape[1:])
    core_ref[0] = core
    sec = mm(test_ref[...], core)
    second_ref[0] = sec
    part = mm_nt(sec, sec)

    @pl.when(step == 0)
    def _():
        gram_ref[:, :width] = part

    @pl.when(step > 0)
    def _():
        gram_ref[:, :width] = gram_ref[:, :width] + part

    @pl.when(step == pl.num_programs(0) - 1)
    def _():
        gram_out_ref[...] = jnp.zeros_like(gram_out_ref)
        gram_out_ref[:width, :] = gram_ref[:, :128]
        gram_out_ref[width : 2 * width, : width - 128] = gram_ref[:, 128:width]


def second_stage(recv, test_t, devices):
    import functools

    parts, groups, ranks, cols_z, lanes = recv.shape
    width, total_z = test_t.shape
    gram_rows = 4 * devices
    return pl.pallas_call(
        functools.partial(second_kernel, width=width),
        grid=(ranks,),
        out_shape=(
            jax.ShapeDtypeStruct((ranks, total_z, lanes), F32),
            jax.ShapeDtypeStruct((ranks, width, lanes), F32),
            jax.ShapeDtypeStruct((gram_rows, 128), F32),
        ),
        in_specs=[
            pl.BlockSpec((parts, groups, 1, cols_z, lanes), lambda i: (0, 0, i, 0, 0)),
            pl.BlockSpec((width, total_z), lambda i: (0, 0)),
        ],
        out_specs=(
            pl.BlockSpec((1, total_z, lanes), lambda i: (i, 0, 0)),
            pl.BlockSpec((1, width, lanes), lambda i: (i, 0, 0)),
            pl.BlockSpec((gram_rows, 128), lambda i: (0, 0)),
        ),
        scratch_shapes=[pltpu.VMEM((width, -(-width // 128) * 128), F32)],
        compiler_params=pltpu.CompilerParams(vmem_limit_bytes=VMEM_LIMIT),
        name="second_stage",
    )(recv, test_t)


def middle_kernel(gram_ref, second_ref, core_ref, q_ref, sums_ref, inv_ref, wide_ref, *, width):
    tiles = [
        [gram_ref[8 * t : 8 * t + 8, :], gram_ref[width + 8 * t : width + 8 * t + 8, :]]
        for t in range(width // 8)
    ]
    put_inverse(tiles, width, inv_ref)
    inv = inv_ref[:, :width]
    total_z = core_ref.shape[1]
    gram = None
    last = None
    for r in range(second_ref.shape[0]):
        q = mm(inv, second_ref[r])
        q_ref[r] = q
        g = mm_nt(q, q)
        h = mm_nt(q, core_ref[r])
        gram = g if gram is None else gram + g
        last = h if last is None else last + h
    wide_ref[:, total_z:] = jnp.zeros((width, wide_ref.shape[1] - total_z), F32)
    wide_ref[:, :total_z] = last
    wide_ref[:, total_z : total_z + width] = gram
    lanes = wide_ref.shape[1] // 128
    for t in range(width // 8):
        for l in range(lanes):
            sums_ref[t * lanes + l] = wide_ref[8 * t : 8 * t + 8, 128 * l : 128 * l + 128]
    for n in range(width // 8 * lanes, sums_ref.shape[0]):
        sums_ref[n] = jnp.zeros((8, 128), F32)


def middle_stage(gram, second, core, devices):
    import functools

    ranks, width, lanes = second.shape
    total_z = core.shape[1]
    wide = total_z + -(-width // 128) * 128
    count = width // 8 * (wide // 128)
    count = -(-count // devices) * devices
    vmem = pl.BlockSpec(memory_space=pltpu.VMEM)
    return pl.pallas_call(
        functools.partial(middle_kernel, width=width),
        out_shape=(
            jax.ShapeDtypeStruct((ranks, width, lanes), F32),
            jax.ShapeDtypeStruct((count, 8, 128), F32),
        ),
        in_specs=[vmem, vmem, vmem],
        out_specs=(vmem, vmem),
        scratch_shapes=[
            pltpu.VMEM((width, -(-width // 128) * 128), F32),
            pltpu.VMEM((width, wide), F32),
        ],
        compiler_params=pltpu.CompilerParams(vmem_limit_bytes=VMEM_LIMIT),
        name="middle_stage",
    )(gram, second, core)


def last_kernel(sums_ref, q_ref, basis_ref, last_ref, inv_ref, wide_ref, *, width, lanes, scales):
    first = last_ref.shape[1] // 128
    tiles = [
        [sums_ref[t * lanes + first + l] for l in range(lanes - first)] for t in range(width // 8)
    ]
    put_inverse(tiles, width, inv_ref)
    inv = inv_ref[:, :width]
    for t in range(width // 8):
        for l in range(first):
            wide_ref[8 * t : 8 * t + 8, 128 * l : 128 * l + 128] = sums_ref[t * lanes + l]
    last_ref[...] = scales[1] * mm(inv, wide_ref[...])
    for r in range(q_ref.shape[0]):
        basis = scales[0] * mm(inv, q_ref[r])
        basis = basis.T
        for m in range(basis_ref.shape[0]):
            rows = basis_ref.shape[2]
            basis_ref[m, r] = basis[m * rows : (m + 1) * rows, :]


def last_stage(sums, q, total_z, members, scales):
    import functools

    ranks, width, span = q.shape
    lanes = (total_z + -(-width // 128) * 128) // 128
    vmem = pl.BlockSpec(memory_space=pltpu.VMEM)
    return pl.pallas_call(
        functools.partial(last_kernel, width=width, lanes=lanes, scales=scales),
        out_shape=(
            jax.ShapeDtypeStruct((members, ranks, span // members, width), F32),
            jax.ShapeDtypeStruct((width, total_z), F32),
        ),
        in_specs=[vmem, vmem],
        out_specs=(vmem, vmem),
        scratch_shapes=[
            pltpu.VMEM((width, -(-width // 128) * 128), F32),
            pltpu.VMEM((width, total_z), F32),
        ],
        compiler_params=pltpu.CompilerParams(vmem_limit_bytes=VMEM_LIMIT),
        name="last_stage",
    )(sums, q)


def swap(pieces, axes, groups=None):
    return lax.all_to_all(pieces, axes, 0, 0, axis_index_groups=groups, tiled=True)


def share(piece, axes, count):
    return swap(jnp.broadcast_to(piece[None], (count,) + piece.shape), axes)


def shards(tensor, factor_y, factor_z, test_matrix):
    rows_x, cols_z, cols_y = tensor.shape
    rank = factor_y.shape[1]
    width = test_matrix.shape[1]
    n_sx = lax.axis_size("sx")
    n_ly = lax.axis_size("ly")
    both = ("sx", "ly")
    devices = n_sx * n_ly
    total_x = rows_x * n_sx
    total_z = cols_z * n_ly
    partial_value = jnp.dot(tensor.reshape(rows_x * cols_z, cols_y), factor_y, precision=HI)
    partial_value = partial_value.reshape(rows_x, cols_z, rank)
    local_sketch = jnp.sum(partial_value * factor_z[None], axis=1)
    mine = jnp.sum(swap(local_sketch.reshape(n_ly, rows_x // n_ly, rank), "ly"), axis=0)
    sketch = share(mine, both, devices).reshape(total_x, rank)
    index = lax.axis_index("sx").astype(jnp.int32).reshape(1)
    qt, basis_t = first_basis(sketch, index, rows_x, math.sqrt(total_x))

    blocks = cols_y // 128
    members = n_ly // blocks
    ranks = rank // (n_sx * members)
    partial_core = product(qt, tensor, n_sx)
    recv = swap(partial_core.reshape(devices, ranks, cols_z, 128), both)
    recv = recv.reshape(n_sx, n_ly, ranks, cols_z, 128)
    core, second, gram = second_stage(recv, test_matrix.T, devices)
    gram = jnp.sum(swap(gram.reshape(devices, 4, 128), both), axis=0)
    gram = share(gram, both, devices).reshape(devices * 4, 128)
    q_one, sums = middle_stage(gram, second, core, devices)
    per = sums.shape[0] // devices
    sums = jnp.sum(swap(sums.reshape(devices, per, 8, 128), both), axis=0)
    sums = share(sums, both, devices).reshape(devices * per, 8, 128)
    scales = (math.sqrt(rank * cols_y), math.sqrt(width / (total_x * cols_y)))
    basis, last_core = last_stage(sums, q_one, total_z, members, scales)
    groups = [[b * members + m for m in range(members)] for b in range(blocks)]
    basis = swap(basis, "ly", groups)
    basis_second = basis.reshape(members * ranks, 128 // members, width)
    return (basis_t.T, basis_second, last_core)


def solution(mesh):
    return jax.shard_map(
        shards,
        mesh=mesh,
        in_specs=(P("sx", "ly", None), P(), P("ly", None), P()),
        out_specs=(P("sx", None), P("sx", "ly", None), P()),
        check_vma=False,
    )
```

profile of v0, /device:TPU:1, one launch (start us, length us, event | category | flops | bytes accessed | tf_op | source)
XLA Modules:
  0.0 393.7 jit_solution(11674742987865874666)
XLA Ops:
  0.6 0.0 copy-start
  0.6 1.0 copy-done
  1.6 19.9 %multiply_reduce_fusion = f32[256,160]{1,0:T(8,128)S(1)} fusion(f32[40,160]{1,0:T(8,128)} %param.6, f32[256,40,512]{2,1,0:T(8,128)} %param.4, f32[512,160]{0,1:T(8,128)S(1)} %copy-done), kind=kOutput, calls=%fused_computation | convolution fusion | flops 10069565440 | bytes 21488640 | tf_op jit(solution)/shard_map/dot_general | solution.py:376
  21.5 18.1 %all_to_all.40 = f32[32,8,160]{2,1,0:T(8,128)S(1)} all-to-all(f32[32,8,160]{2,1,0:T(8,128)S(1)} %bitcast.23), channel_id=1, replica_groups=mesh['sx'=4,'ly'=32] {'ly'}, dimensions={0} | all-to-all | bytes 327680 | tf_op jit(solution)/shard_map/all_to_all | solution.py:359
  39.6 1.1 broadcast_in_dim.6
  40.7 6.1 %all-to-all-start.1 = ((f32[128,8,160]{2,1,0:T(8,128)}), f32[128,8,160]{2,1,0:T(8,128)S(1)}, u32[]{:S(2)}, u32[]{:S(2)}) async-start(f32[128,8,160]{2,1,0:T(8,128)} %broadcast_in_dim.6), calls=%async_computation.1 | async-start | bytes 2097152 | tf_op jit(solution)/shard_map/all_to_all | solution.py:359
  46.8 19.1 %all-to-all-done.1 = f32[128,8,160]{2,1,0:T(8,128)S(1)} async-done(((f32[128,8,160]{2,1,0:T(8,128)}), f32[128,8,160]{2,1,0:T(8,128)S(1)}, u32[]{:S(2)}, u32[]{:S(2)}) %all-to-all-start.1) | async-done | bytes 655392 | tf_op jit(solution)/shard_map/all_to_all | solution.py:359
  65.9 0.0 copy-start.1
  65.9 1.0 copy-done.1
  66.9 18.0 %first_basis.1 = (f32[160,256]{1,0:T(8,128)}, f32[160,256]{1,0:T(8,128)}) custom-call(s32[1]{0:T(128)} %bitcast.index_ref, f32[1024,160]{1,0:T(8,128)} %bitcast.20), custom_call_target="tpu_custom_call" | custom-call | tf_op jit(solution)/shard_map/first_basis/pallas_call | solution.py:128
  85.0 18.3 %product.1 = f32[4,4,1600,128]{3,2,1,0:T(8,128)} custom-call(f32[160,256]{1,0:T(8,128)} %get-tuple-element.13.qt_ref, f32[10240,512]{1,0:T(8,128)} %bitcast.17), custom_call_target="tpu_custom_call" | custom-call | tf_op jit(solution)/shard_map/product/pallas_call | solution.py:191
  103.3 154.3 %all_to_all.41 = f32[128,5,40,128]{3,2,1,0:T(8,128)} all-to-all(f32[128,5,40,128]{3,2,1,0:T(8,128)} %bitcast.19), channel_id=1, replica_groups=mesh['sx'=4,'ly'=32] {'sx','ly'}, dimensions={0} | all-to-all | bytes 26214400 | tf_op jit(solution)/shard_map/all_to_all | solution.py:359
  257.5 11.2 %second_stage.1 = (f32[5,1280,128]{2,1,0:T(8,128)}, f32[5,160,128]{2,1,0:T(8,128)}, f32[512,128]{1,0:T(8,128)}) custom-call(f32[4,32,5,40,128]{4,3,2,1,0:T(8,128)} %bitcast.18, f32[160,1280]{1,0:T(8,128)} %bitcast.26), custom_call_target="tpu_custom_call" | custom-call | tf_op jit(solution)/shard_map/second_stage/pallas_call | solution.py:239
  268.8 19.6 %all_to_all.42 = f32[128,4,128]{2,1,0:T(4,128)S(1)} all-to-all(f32[128,4,128]{2,1,0:T(4,128)} %bitcast.27), channel_id=1, replica_groups=mesh['sx'=4,'ly'=32] {'sx','ly'}, dimensions={0} | all-to-all | bytes 524288 | tf_op jit(solution)/shard_map/all_to_all | solution.py:359
  288.4 0.1 reduce_sum.38
  288.6 15.3 %all_to_all.43 = f32[128,4,128]{2,1,0:T(4,128)} all-to-all(f32[128,4,128]{2,1,0:T(4,128)S(1)} %broadcast_in_dim.7), channel_id=1, replica_groups=mesh['sx'=4,'ly'=32] {'sx','ly'}, dimensions={0} | all-to-all | bytes 524288 | tf_op jit(solution)/shard_map/all_to_all | solution.py:359
  303.9 15.0 %middle_stage.1 = (f32[5,160,128]{2,1,0:T(8,128)}, f32[256,8,128]{2,1,0:T(8,128)}) custom-call(f32[512,128]{1,0:T(8,128)} %bitcast.25, f32[5,160,128]{2,1,0:T(8,128)} %get-tuple-element.15.second_ref, f32[5,1280,128]{2,1,0:T(8,128)} %get-tuple-element.16.core_ref), custom_call_target="tpu_custom_call" | custom-call | tf_op jit(solution)/shard_map/middle_stage/pallas_call | solution.py:299
  318.9 24.1 %all_to_all.44 = f32[128,2,8,128]{3,2,1,0:T(8,128)S(1)} all-to-all(f32[128,2,8,128]{3,2,1,0:T(8,128)} %bitcast.24), channel_id=1, replica_groups=mesh['sx'=4,'ly'=32] {'sx','ly'}, dimensions={0} | all-to-all | bytes 2097152 | tf_op jit(solution)/shard_map/all_to_all | solution.py:359
  343.0 0.1 reduce_sum.39
  343.1 0.1 broadcast_in_dim.8
  343.2 23.8 %all_to_all.45 = f32[128,2,8,128]{3,2,1,0:T(8,128)} all-to-all(f32[128,2,8,128]{3,2,1,0:T(8,128)S(1)} %broadcast_in_dim.8), channel_id=1, replica_groups=mesh['sx'=4,'ly'=32] {'sx','ly'}, dimensions={0} | all-to-all | bytes 2097152 | tf_op jit(solution)/shard_map/all_to_all | solution.py:359
  367.0 10.1 %last_stage.1 = (f32[8,5,16,160]{3,2,1,0:T(8,128)}, f32[160,1280]{1,0:T(8,128)}) custom-call(f32[256,8,128]{2,1,0:T(8,128)} %bitcast.21, f32[5,160,128]{2,1,0:T(8,128)} %get-tuple-element.18.q_ref), custom_call_target="tpu_custom_call" | custom-call | tf_op jit(solution)/shard_map/last_stage/pallas_call | solution.py:341
  377.2 15.3 %all_to_all.46 = f32[8,5,16,160]{3,2,1,0:T(8,128)S(1)} all-to-all(f32[8,5,16,160]{3,2,1,0:T(8,128)} %get-tuple-element.19), channel_id=1, replica_groups={{0,1,2,3,4,5,6,7},{8,9,10,11,12,13,14,15},{16,17,18,19,20,21,22,23},{24..., dimensions={0} | all-to-all | bytes 819200 | tf_op jit(solution)/shard_map/all_to_all | solution.py:359
  392.5 0.8 copy.13
  (2 shorter events, 0.1 us)
Async XLA Ops:
  0.6 1.0 copy-start
  40.7 25.2 %all-to-all-start.1 = ((f32[128,8,160]{2,1,0:T(8,128)}), f32[128,8,160]{2,1,0:T(8,128)S(1)}, u32[]{:S(2)}, u32[]{:S(2)}) async-start(f32[128,8,160]{2,1,0:T(8,128)} %broadcast_in_dim.6), calls=%async_computation.1 | async-start | bytes 2097152 | tf_op jit(solution)/shard_map/all_to_all | solution.py:359
  65.9 1.0 copy-start.1
where the time goes:
time: 399 us; the launch traced here: 394 us
  blocking collectives  271 us (68%)
  Pallas kernels  72.7 us (18%)
  matrix products  19.9 us (5%)
  waiting for transfers between devices  19.1 us (5%)
  starting transfers between devices  6.1 us (2%)
    all_to_all x7, blocking collectives, swap(): lax.all_to_all(pieces, axes, 0, 0, axis_index_groups=groups, tiled=True)  271 us
    dot_general x1, matrix products, shards(): jnp.dot(tensor.reshape(rows_x * cols_z, cols_y), factor_y, precision=HI)  19.9 us
    all_to_all x1, waiting for transfers between devices, swap(): lax.all_to_all(pieces, axes, 0, 0, axis_index_groups=groups, tiled=True)  19.1 us
    pallas_call x1, Pallas kernels, product(): pl.pallas_call(functools.partial(product_kernel, cols_z=cols_z, rows_x=ro...  18.3 us
    pallas_call x1, Pallas kernels, first_basis(): pl.pallas_call(functools.partial(first_kernel, rank=rank, rows_x=rows_x,...  18 us
    pallas_call x1, Pallas kernels, middle_stage(): pl.pallas_call(functools.partial(middle_kernel, width=width), out_shape=(...  15 us
    pallas_call x1, Pallas kernels, second_stage(): pl.pallas_call(functools.partial(second_kernel, width=width), grid=(ranks...  11.2 us
    pallas_call x1, Pallas kernels, last_stage(): pl.pallas_call(functools.partial(last_kernel, width=width, lanes=lanes, s...  10.1 us
  transfers between devices with their start and end apart: 1, of which 1 were waited for; matrix products, arithmetic and copies ran while one was open for 0% of the time, Pallas kernels for 0%

commit v1 on v0

--- a/solution.py
+++ b/solution.py
@@ -1,3 +1,4 @@
+import functools
 import math
 
 import jax
@@ -10,14 +11,7 @@
 HI = lax.Precision.HIGHEST
 F32 = jnp.float32
 VMEM_LIMIT = 56 * 1024 * 1024
-
-
-def mm(a, b):
-    return lax.dot_general(a, b, (((1,), (0,)), ((), ())), precision=HI, preferred_element_type=F32)
-
-
-def mm_nt(a, b):
-    return lax.dot_general(a, b, (((1,), (1,)), ((), ())), precision=HI, preferred_element_type=F32)
+UNROLL = 4
 
 
 GROUP = 5
@@ -30,8 +24,10 @@
         for t in range(size // 8)
     ]
 
+
 def spread(row, tile):
     return jnp.broadcast_to(tile[row : row + 1, :], (8, 128))
+
 
 def put_inverse(tiles, size, out_ref, group=GROUP):
     count = size // 8
@@ -101,32 +97,64 @@
                     work[t][l] = old - outer[8 * t : 8 * t + 8, 128 * l : 128 * l + 128]
 
 
-def first_kernel(index_ref, sketch_ref, q_ref, basis_ref, gram_ref, inv_ref, qt_ref, *, rank, rows_x, scale):
-    sk = sketch_ref[...]
+def split(value):
+    high = value.astype(jnp.bfloat16)
+    rest = value - high.astype(F32)
+    middle = rest.astype(jnp.bfloat16)
+    low = (rest - middle.astype(F32)).astype(jnp.bfloat16)
+    return high, middle, low
+
+
+def dot_bf16(a, b):
+    return lax.dot_general(a, b, (((1,), (0,)), ((), ())), preferred_element_type=F32)
+
+
+def dot_six(a, b, transposed=False):
+    rows = a.shape[0]
+    dims = (((1,), (1 if transposed else 0,)), ((), ()))
+    left = jnp.concatenate(split(a), axis=0)
+    high, middle, low = split(b)
+
+    def dot(x, y):
+        return lax.dot_general(x, y, dims, preferred_element_type=F32)
+
+    first = dot(left, high)
+    second = dot(left[: 2 * rows], middle)
+    third = dot(left[:rows], low)
+    return first[:rows] + (
+        (first[rows : 2 * rows] + second[:rows]) + (first[2 * rows :] + (second[rows:] + third))
+    )
+
+
+def first_kernel(index_ref, sketch_ref, q_ref, basis_ref, gram_ref, inv_ref, wide_ref, *, rank, scale):
+    rows_x = q_ref.shape[1]
+    total = wide_ref.shape[1]
+    halves = rows_x // 128
+    for n in range(total // 128):
+        block, half = divmod(n, halves)
+        rows = pl.ds(block * rank * halves + half, rank, stride=halves)
+        wide_ref[:, 128 * n : 128 * n + 128] = sketch_ref[rows, :]
     gram_ref[...] = jnp.zeros_like(gram_ref)
-    gram_ref[:, :rank] = lax.dot_general(
-        sk, sk, (((0,), (0,)), ((), ())), precision=HI, preferred_element_type=F32
-    )
+    sketch = wide_ref[...]
+    gram_ref[:, :rank] = dot_six(sketch, sketch, True)
     put_inverse(tiles_of(gram_ref, rank), rank, inv_ref)
-    qt = mm_nt(inv_ref[:, :rank], sk)
-    qt_ref[...] = qt
-    gram_ref[:, :rank] = mm_nt(qt, qt)
+    qt = dot_six(inv_ref[:, :rank], sketch)
+    wide_ref[...] = qt
+    gram_ref[:, :rank] = dot_six(qt, qt, True)
     put_inverse(tiles_of(gram_ref, rank), rank, inv_ref)
     at = pl.multiple_of(index_ref[0] * rows_x, 128)
-    mine = mm(inv_ref[:, :rank], qt_ref[:, pl.ds(at, rows_x)])
+    mine = dot_six(inv_ref[:, :rank], wide_ref[:, pl.ds(at, rows_x)])
     q_ref[...] = mine
     basis_ref[...] = scale * mine
 
 
-def first_basis(sketch, index, rows_x, scale):
-    total, rank = sketch.shape
+def first_basis(sketch, index, rank, rows_x, scale):
+    total = sketch.shape[0] * 128 // rank
     wide = -(-rank // 128) * 128
     shape = jax.ShapeDtypeStruct((rank, rows_x), F32)
-    import functools
-
     vmem = pl.BlockSpec(memory_space=pltpu.VMEM)
     return pl.pallas_call(
-        functools.partial(first_kernel, rank=rank, rows_x=rows_x, scale=scale),
+        functools.partial(first_kernel, rank=rank, scale=scale),
         out_shape=(shape, shape),
         in_specs=[pl.BlockSpec(memory_space=pltpu.SMEM), vmem],
         out_specs=(vmem, vmem),
@@ -140,16 +168,76 @@
     )(index, sketch)
 
 
-def split(value):
-    high = value.astype(jnp.bfloat16)
-    rest = value - high.astype(F32)
-    middle = rest.astype(jnp.bfloat16)
-    low = (rest - middle.astype(F32)).astype(jnp.bfloat16)
-    return high, middle, low
-
-
-def dot_bf16(a, b):
-    return lax.dot_general(a, b, (((1,), (0,)), ((), ())), preferred_element_type=F32)
+def sketch_kernel(*refs):
+    slab_refs, (fy_ref, fz_ref, out_ref, left_ref, sum_ref) = refs[:-5], refs[-5:]
+    step = pl.program_id(0)
+    rows_x, span, lanes = slab_refs[0].shape
+    rank = fy_ref.shape[0]
+    flat = [ref.reshape(rows_x * span, lanes) for ref in slab_refs]
+
+    @pl.when(step == 0)
+    def _():
+        for n, piece in enumerate(split(fy_ref[...])):
+            left_ref[n * rank : (n + 1) * rank, :] = piece
+
+    def dot(x, y):
+        dims = (((1,), (1,)), ((), ()))
+        return lax.dot_general(x, y, dims, preferred_element_type=F32)
+
+    total = None
+    for i in range(span):
+        rows = pl.ds(i, rows_x, stride=span)
+        high, middle, low = split(jnp.concatenate([ref[rows, :] for ref in flat], axis=1))
+        first = dot(left_ref[...], high)
+        second = dot(left_ref[: 2 * rank, :], middle)
+        third = dot(left_ref[:rank, :], low)
+        part = first[:rank] + (
+            (first[rank : 2 * rank] + second[:rank]) + (first[2 * rank :] + (second[rank:] + third))
+        )
+        part = part * fz_ref[0, :, i : i + 1]
+        total = part if total is None else total + part
+
+    @pl.when(step == 0)
+    def _():
+        sum_ref[...] = total
+
+    @pl.when(step > 0)
+    def _():
+        sum_ref[...] = sum_ref[...] + total
+
+    @pl.when(step == pl.num_programs(0) - 1)
+    def _():
+        halves = rows_x // 128
+        for n in range(halves):
+            out_ref[pl.ds(n, rank, stride=halves), :] = sum_ref[:, 128 * n : 128 * n + 128]
+
+
+def local_sketch(tensor, fy_t, factor_z):
+    rows_x, cols_z, cols_y = tensor.shape
+    rank = fy_t.shape[0]
+    steps = cols_z // 8
+    blocks = cols_y // 128
+    fz = factor_z.reshape(steps, 8, rank).transpose(0, 2, 1)
+    return pl.pallas_call(
+        sketch_kernel,
+        grid=(steps,),
+        out_shape=jax.ShapeDtypeStruct((rank * rows_x // 128, 128), F32),
+        in_specs=[
+            *(
+                pl.BlockSpec((rows_x, 8, 128), functools.partial(lambda l, i: (0, i, l), l))
+                for l in range(blocks)
+            ),
+            pl.BlockSpec((rank, cols_y), lambda i: (0, 0)),
+            pl.BlockSpec((1, rank, 8), lambda i: (i, 0, 0)),
+        ],
+        out_specs=pl.BlockSpec((rank * rows_x // 128, 128), lambda i: (0, 0)),
+        scratch_shapes=[
+            pltpu.VMEM((3 * rank, cols_y), jnp.bfloat16),
+            pltpu.VMEM((rank, rows_x), F32),
+        ],
+        compiler_params=pltpu.CompilerParams(vmem_limit_bytes=VMEM_LIMIT),
+        name="local_sketch",
+    )(*[tensor] * blocks, fy_t, fz)
 
 
 def product_kernel(qt_ref, slab_ref, out_ref, left_ref, *, cols_z, rows_x, parts, rank_part):
@@ -177,12 +265,10 @@
             out_ref[s, 0, pl.ds(z + 1, rank_part, stride=cols_z), :] = piece[:, 128:]
         return carry
 
-    lax.fori_loop(0, cols_z // 2, body, 0, unroll=10)
+    lax.fori_loop(0, cols_z // 2, body, 0, unroll=UNROLL)
 
 
 def product(qt, tensor, parts):
-    import functools
-
     rows_x, cols_z, cols_y = tensor.shape
     rank = qt.shape[0]
     blocks = cols_y // 128
@@ -209,11 +295,11 @@
     step = pl.program_id(0)
     core = recv_ref[0, :, 0] + recv_ref[1, :, 0]
     core = core + (recv_ref[2, :, 0] + recv_ref[3, :, 0])
-    core = core.reshape(core_ref.shape[1:])
-    core_ref[0] = core
-    sec = mm(test_ref[...], core)
-    second_ref[0] = sec
-    part = mm_nt(sec, sec)
+    core = core.reshape(core_ref.shape)
+    core_ref[...] = core
+    sec = dot_six(test_ref[...], core)
+    second_ref[...] = sec
+    part = dot_six(sec, sec, True)
 
     @pl.when(step == 0)
     def _():
@@ -231,8 +317,6 @@
 
 
 def second_stage(recv, test_t, devices):
-    import functools
-
     parts, groups, ranks, cols_z, lanes = recv.shape
     width, total_z = test_t.shape
     gram_rows = 4 * devices
@@ -240,8 +324,8 @@
         functools.partial(second_kernel, width=width),
         grid=(ranks,),
         out_shape=(
-            jax.ShapeDtypeStruct((ranks, total_z, lanes), F32),
-            jax.ShapeDtypeStruct((ranks, width, lanes), F32),
+            jax.ShapeDtypeStruct((total_z, ranks * lanes), F32),
+            jax.ShapeDtypeStruct((width, ranks * lanes), F32),
             jax.ShapeDtypeStruct((gram_rows, 128), F32),
         ),
         in_specs=[
@@ -249,8 +333,8 @@
             pl.BlockSpec((width, total_z), lambda i: (0, 0)),
         ],
         out_specs=(
-            pl.BlockSpec((1, total_z, lanes), lambda i: (i, 0, 0)),
-            pl.BlockSpec((1, width, lanes), lambda i: (i, 0, 0)),
+            pl.BlockSpec((total_z, lanes), lambda i: (0, i)),
+            pl.BlockSpec((width, lanes), lambda i: (0, i)),
             pl.BlockSpec((gram_rows, 128), lambda i: (0, 0)),
         ),
         scratch_shapes=[pltpu.VMEM((width, -(-width // 128) * 128), F32)],
@@ -265,20 +349,16 @@
         for t in range(width // 8)
     ]
     put_inverse(tiles, width, inv_ref)
-    inv = inv_ref[:, :width]
-    total_z = core_ref.shape[1]
-    gram = None
-    last = None
-    for r in range(second_ref.shape[0]):
-        q = mm(inv, second_ref[r])
-        q_ref[r] = q
-        g = mm_nt(q, q)
-        h = mm_nt(q, core_ref[r])
-        gram = g if gram is None else gram + g
-        last = h if last is None else last + h
+    total_z = core_ref.shape[0]
+    q = dot_six(inv_ref[:, :width], second_ref[...])
+    members, ranks, rows, _ = q_ref.shape
+    for r in range(ranks):
+        turned = q[:, r * members * rows : (r + 1) * members * rows].T
+        for m in range(members):
+            q_ref[m, r] = turned[m * rows : (m + 1) * rows, :]
     wide_ref[:, total_z:] = jnp.zeros((width, wide_ref.shape[1] - total_z), F32)
-    wide_ref[:, :total_z] = last
-    wide_ref[:, total_z : total_z + width] = gram
+    wide_ref[:, :total_z] = dot_six(q, core_ref[...], True)
+    wide_ref[:, total_z : total_z + width] = dot_six(q, q, True)
     lanes = wide_ref.shape[1] // 128
     for t in range(width // 8):
         for l in range(lanes):
@@ -287,11 +367,9 @@
         sums_ref[n] = jnp.zeros((8, 128), F32)
 
 
-def middle_stage(gram, second, core, devices):
-    import functools
-
-    ranks, width, lanes = second.shape
-    total_z = core.shape[1]
+def middle_stage(gram, second, core, devices, ranks, members):
+    width, pairs = second.shape
+    total_z = core.shape[0]
     wide = total_z + -(-width // 128) * 128
     count = width // 8 * (wide // 128)
     count = -(-count // devices) * devices
@@ -299,7 +377,7 @@
     return pl.pallas_call(
         functools.partial(middle_kernel, width=width),
         out_shape=(
-            jax.ShapeDtypeStruct((ranks, width, lanes), F32),
+            jax.ShapeDtypeStruct((members, ranks, pairs // ranks // members, width), F32),
             jax.ShapeDtypeStruct((count, 8, 128), F32),
         ),
         in_specs=[vmem, vmem, vmem],
@@ -313,46 +391,49 @@
     )(gram, second, core)
 
 
-def last_kernel(sums_ref, q_ref, basis_ref, last_ref, inv_ref, wide_ref, *, width, lanes, scales):
+def last_kernel(sums_ref, last_ref, inv_ref, wide_ref, *, width, lanes, scale):
     first = last_ref.shape[1] // 128
     tiles = [
         [sums_ref[t * lanes + first + l] for l in range(lanes - first)] for t in range(width // 8)
     ]
     put_inverse(tiles, width, inv_ref)
-    inv = inv_ref[:, :width]
     for t in range(width // 8):
         for l in range(first):
             wide_ref[8 * t : 8 * t + 8, 128 * l : 128 * l + 128] = sums_ref[t * lanes + l]
-    last_ref[...] = scales[1] * mm(inv, wide_ref[...])
-    for r in range(q_ref.shape[0]):
-        basis = scales[0] * mm(inv, q_ref[r])
-        basis = basis.T
-        for m in range(basis_ref.shape[0]):
-            rows = basis_ref.shape[2]
-            basis_ref[m, r] = basis[m * rows : (m + 1) * rows, :]
-
-
-def last_stage(sums, q, total_z, members, scales):
-    import functools
-
-    ranks, width, span = q.shape
-    lanes = (total_z + -(-width // 128) * 128) // 128
+    last_ref[...] = scale * dot_six(inv_ref[:, :width], wide_ref[...])
+
+
+def last_stage(sums, total_z, width, scale):
+    wide = -(-width // 128) * 128
     vmem = pl.BlockSpec(memory_space=pltpu.VMEM)
     return pl.pallas_call(
-        functools.partial(last_kernel, width=width, lanes=lanes, scales=scales),
+        functools.partial(last_kernel, width=width, lanes=(total_z + wide) // 128, scale=scale),
         out_shape=(
-            jax.ShapeDtypeStruct((members, ranks, span // members, width), F32),
             jax.ShapeDtypeStruct((width, total_z), F32),
+            jax.ShapeDtypeStruct((width, wide), F32),
         ),
+        in_specs=[vmem],
+        out_specs=(vmem, vmem),
+        scratch_shapes=[pltpu.VMEM((width, total_z), F32)],
+        compiler_params=pltpu.CompilerParams(vmem_limit_bytes=VMEM_LIMIT),
+        name="last_stage",
+    )(sums)
+
+
+def basis_kernel(q_ref, inv_ref, basis_ref, *, scale):
+    basis_ref[...] = scale * dot_six(q_ref[...], inv_ref[:, : q_ref.shape[1]], True)
+
+
+def basis_stage(q, inverse, scale):
+    vmem = pl.BlockSpec(memory_space=pltpu.VMEM)
+    return pl.pallas_call(
+        functools.partial(basis_kernel, scale=scale),
+        out_shape=jax.ShapeDtypeStruct(q.shape, F32),
         in_specs=[vmem, vmem],
-        out_specs=(vmem, vmem),
-        scratch_shapes=[
-            pltpu.VMEM((width, -(-width // 128) * 128), F32),
-            pltpu.VMEM((width, total_z), F32),
-        ],
-        compiler_params=pltpu.CompilerParams(vmem_limit_bytes=VMEM_LIMIT),
-        name="last_stage",
-    )(sums, q)
+        out_specs=vmem,
+        compiler_params=pltpu.CompilerParams(vmem_limit_bytes=VMEM_LIMIT),
+        name="basis_stage",
+    )(q, inverse)
 
 
 def swap(pieces, axes, groups=None):
@@ -373,13 +454,13 @@
     devices = n_sx * n_ly
     total_x = rows_x * n_sx
     total_z = cols_z * n_ly
-    partial_value = jnp.dot(tensor.reshape(rows_x * cols_z, cols_y), factor_y, precision=HI)
-    partial_value = partial_value.reshape(rows_x, cols_z, rank)
-    local_sketch = jnp.sum(partial_value * factor_z[None], axis=1)
-    mine = jnp.sum(swap(local_sketch.reshape(n_ly, rows_x // n_ly, rank), "ly"), axis=0)
-    sketch = share(mine, both, devices).reshape(total_x, rank)
+    halves = rows_x // 128
+    local = local_sketch(tensor, factor_y.T, factor_z)
+    local = swap(local.reshape(rank, halves, 128), "ly")
+    mine = jnp.sum(local.reshape(n_ly, rank // n_ly, halves, 128), axis=0)
+    sketch = share(mine, both, devices).reshape(n_sx * rank * halves, 128)
     index = lax.axis_index("sx").astype(jnp.int32).reshape(1)
-    qt, basis_t = first_basis(sketch, index, rows_x, math.sqrt(total_x))
+    qt, basis_t = first_basis(sketch, index, rank, rows_x, math.sqrt(total_x))
 
     blocks = cols_y // 128
     members = n_ly // blocks
@@ -390,15 +471,19 @@
     core, second, gram = second_stage(recv, test_matrix.T, devices)
     gram = jnp.sum(swap(gram.reshape(devices, 4, 128), both), axis=0)
     gram = share(gram, both, devices).reshape(devices * 4, 128)
-    q_one, sums = middle_stage(gram, second, core, devices)
+    q_one, sums = middle_stage(gram, second, core, devices, ranks, members)
+    groups = [[b * members + m for m in range(members)] for b in range(blocks)]
+    q_mine = swap(q_one, "ly", groups)
+    q_mine = q_mine.reshape(rank // n_sx * (128 // members), width)
     per = sums.shape[0] // devices
-    sums = jnp.sum(swap(sums.reshape(devices, per, 8, 128), both), axis=0)
-    sums = share(sums, both, devices).reshape(devices * per, 8, 128)
-    scales = (math.sqrt(rank * cols_y), math.sqrt(width / (total_x * cols_y)))
-    basis, last_core = last_stage(sums, q_one, total_z, members, scales)
-    groups = [[b * members + m for m in range(members)] for b in range(blocks)]
-    basis = swap(basis, "ly", groups)
-    basis_second = basis.reshape(members * ranks, 128 // members, width)
+    sums = swap(sums.reshape(devices, per, 8, 128), both)
+    sums = jnp.sum(sums, axis=0)
+    sums = share(sums, both, devices)
+    sums = sums.reshape(devices * per, 8, 128)
+    core_scale = math.sqrt(width / (total_x * cols_y))
+    last_core, inverse = last_stage(sums, total_z, width, core_scale)
+    basis = basis_stage(q_mine, inverse, math.sqrt(rank * cols_y))
+    basis_second = basis.reshape(rank // n_sx, 128 // members, width)
     return (basis_t.T, basis_second, last_core)
 
 

time: 399 us -> 379 us (0.950); the launches traced: 394 us -> 378 us
  matrix products: 19.9 us -> 0 us
  Pallas kernels: 72.7 us -> 91.8 us
  blocking collectives: 271 us -> 254 us
  starting transfers between devices: 6.1 us -> 10.3 us
    dot_general x1 -> x0, matrix products: 19.9 us -> none  [shards(): jnp.dot(tensor.reshape(rows_x * cols_z, cols_y), factor_y, precision=HI)]
    pallas_call x2 -> x4, Pallas kernels: 28.2 us -> 47.9 us  [the longest x1 18.2 us: local_sketch(): pl.pallas_call(sketch_kernel, grid=(steps,), out_shape=jax.ShapeDtypeStru...]
    all_to_all x7 -> x6, blocking collectives: 271 us -> 254 us  [swap(): lax.all_to_all(pieces, axes, 0, 0, axis_index_groups=groups, tiled=True)]
    all_to_all x1 -> x2, starting transfers between devices: 6.1 us -> 10.3 us  [swap(): lax.all_to_all(pieces, axes, 0, 0, axis_index_groups=groups, tiled=True)]
    all_to_all x1 -> x2, waiting for transfers between devices: 19.1 us -> 16.4 us  [swap(): lax.all_to_all(pieces, axes, 0, 0, axis_index_groups=groups, tiled=True)]
  transfers between devices with their start and end apart: 1 -> 2, of which waited for: 1 -> 2; matrix products, arithmetic and copies ran while one was open for 0% -> 0% of each run, Pallas kernels for 0% -> 2%
where the time goes in v1:
time: 379 us; the launch traced here: 378 us
  blocking collectives  254 us (67%)
  Pallas kernels  91.8 us (24%)
  waiting for transfers between devices  16.4 us (4%)
  starting transfers between devices  10.3 us (3%)
  local copies, waits for them, and re-layouts  4.51 us (1%)
    all_to_all x6, blocking collectives, swap(): lax.all_to_all(pieces, axes, 0, 0, axis_index_groups=groups, tiled=True)  254 us
    pallas_call x1, Pallas kernels, product(): pl.pallas_call(functools.partial(product_kernel, cols_z=cols_z, rows_x=ro...  20 us
    pallas_call x1, Pallas kernels, local_sketch(): pl.pallas_call(sketch_kernel, grid=(steps,), out_shape=jax.ShapeDtypeStru...  18.2 us
    pallas_call x1, Pallas kernels, first_basis(): pl.pallas_call(functools.partial(first_kernel, rank=rank, scale=scale), o...  17.7 us
    all_to_all x2, waiting for transfers between devices, swap(): lax.all_to_all(pieces, axes, 0, 0, axis_index_groups=groups, tiled=True)  16.4 us
    pallas_call x1, Pallas kernels, middle_stage(): pl.pallas_call(functools.partial(middle_kernel, width=width), out_shape=(...  12.7 us
    pallas_call x1, Pallas kernels, second_stage(): pl.pallas_call(functools.partial(second_kernel, width=width), grid=(ranks...  11.1 us
    all_to_all x2, starting transfers between devices, swap(): lax.all_to_all(pieces, axes, 0, 0, axis_index_groups=groups, tiled=True)  10.3 us
  transfers between devices with their start and end apart: 2, of which 2 were waited for; matrix products, arithmetic and copies ran while one was open for 0% of the time, Pallas kernels for 2%

profile of v1, /device:TPU:1, one launch (start us, length us, event | category | flops | bytes accessed | tf_op | source)
XLA Modules:
  0.0 378.1 jit_solution(15604962237719425731)
XLA Ops:
  0.6 1.7 copy.7
  2.4 18.2 %local_sketch.1 = f32[320,128]{1,0:T(8,128)} custom-call(f32[256,40,512]{2,1,0:T(8,128)} %refs_3_.1, f32[256,40,512]{2,1,0:T(8,128)} %refs_3_.1, f32[256,40,512]{2,1,0:T(8,128)} %refs_3_.1, f32[256,40,512]{2,1,0:T(8,128)} %refs_3_.1, f32[160,512]{1,0:T(8,128)} %bitcast.31, f32[5,160,8]{2,1,0:T(8,128)} %bitcast.24), custom_call_target="tpu_custom_call" | custom-call | tf_op jit(solution)/shard_map/local_sketch/pallas_call | solution.py:221
  20.5 17.3 %all_to_all.40 = f32[160,2,128]{2,1,0:T(2,128)S(1)} all-to-all(f32[160,2,128]{2,1,0:T(2,128)} %bitcast.28), channel_id=1, replica_groups=mesh['sx'=4,'ly'=32] {'ly'}, dimensions={0} | all-to-all | bytes 327680 | tf_op jit(solution)/shard_map/all_to_all | solution.py:440
  37.9 0.1 reduce_sum.27
  38.0 1.0 broadcast_in_dim.6
  39.0 5.9 %all-to-all-start.1 = ((f32[128,5,2,128]{3,2,1,0:T(2,128)}), f32[128,5,2,128]{3,2,1,0:T(2,128)S(1)}, u32[]{:S(2)}, u32[]{:S(2)}) async-start(f32[128,5,2,128]{3,2,1,0:T(2,128)} %broadcast_in_dim.6), calls=%async_computation.1 | async-start | bytes 1310720 | tf_op jit(solution)/shard_map/all_to_all | solution.py:440
  44.9 15.0 %all-to-all-done.1 = f32[128,5,2,128]{3,2,1,0:T(2,128)S(1)} async-done(((f32[128,5,2,128]{3,2,1,0:T(2,128)}), f32[128,5,2,128]{3,2,1,0:T(2,128)S(1)}, u32[]{:S(2)}, u32[]{:S(2)}) %all-to-all-start.1) | async-done | bytes 655392 | tf_op jit(solution)/shard_map/all_to_all | solution.py:440
  59.9 0.0 copy-start
  59.9 0.8 copy-done
  60.7 17.7 %first_basis.1 = (f32[160,256]{1,0:T(8,128)}, f32[160,256]{1,0:T(8,128)}) custom-call(s32[1]{0:T(128)} %bitcast.index_ref, f32[1280,128]{1,0:T(8,128)} %bitcast.22), custom_call_target="tpu_custom_call" | custom-call | tf_op jit(solution)/shard_map/first_basis/pallas_call | solution.py:156
  78.4 20.0 %product.1 = f32[4,4,1600,128]{3,2,1,0:T(8,128)} custom-call(f32[160,256]{1,0:T(8,128)} %get-tuple-element.13.qt_ref, f32[10240,512]{1,0:T(8,128)} %bitcast.18), custom_call_target="tpu_custom_call" | custom-call | tf_op jit(solution)/shard_map/product/pallas_call | solution.py:277
  98.5 154.1 %all_to_all.41 = f32[128,5,40,128]{3,2,1,0:T(8,128)} all-to-all(f32[128,5,40,128]{3,2,1,0:T(8,128)} %bitcast.20), channel_id=1, replica_groups=mesh['sx'=4,'ly'=32] {'sx','ly'}, dimensions={0} | all-to-all | bytes 26214400 | tf_op jit(solution)/shard_map/all_to_all | solution.py:440
  252.6 11.1 %second_stage.1 = (f32[1280,640]{1,0:T(8,128)}, f32[160,640]{1,0:T(8,128)}, f32[512,128]{1,0:T(8,128)}) custom-call(f32[4,32,5,40,128]{4,3,2,1,0:T(8,128)} %bitcast.19, f32[160,1280]{1,0:T(8,128)} %bitcast.27), custom_call_target="tpu_custom_call" | custom-call | tf_op jit(solution)/shard_map/second_stage/pallas_call | solution.py:323
  263.7 19.6 %all_to_all.42 = f32[128,4,128]{2,1,0:T(4,128)S(1)} all-to-all(f32[128,4,128]{2,1,0:T(4,128)} %bitcast.32), channel_id=1, replica_groups=mesh['sx'=4,'ly'=32] {'sx','ly'}, dimensions={0} | all-to-all | bytes 524288 | tf_op jit(solution)/shard_map/all_to_all | solution.py:440
  283.3 0.1 reduce_sum.28
  283.5 15.3 %all_to_all.43 = f32[128,4,128]{2,1,0:T(4,128)} all-to-all(f32[128,4,128]{2,1,0:T(4,128)S(1)} %broadcast_in_dim.7), channel_id=1, replica_groups=mesh['sx'=4,'ly'=32] {'sx','ly'}, dimensions={0} | all-to-all | bytes 524288 | tf_op jit(solution)/shard_map/all_to_all | solution.py:440
  298.8 12.7 %middle_stage.1 = (f32[8,5,16,160]{3,2,1,0:T(8,128)}, f32[256,8,128]{2,1,0:T(8,128)}) custom-call(f32[512,128]{1,0:T(8,128)} %bitcast.26, f32[160,640]{1,0:T(8,128)} %get-tuple-element.15.second_ref, f32[1280,640]{1,0:T(8,128)} %get-tuple-element.16.core_ref), custom_call_target="tpu_custom_call" | custom-call | tf_op jit(solution)/shard_map/middle_stage/pallas_call | solution.py:377
  311.5 23.9 %all_to_all.44 = f32[128,2,8,128]{3,2,1,0:T(8,128)S(1)} all-to-all(f32[128,2,8,128]{3,2,1,0:T(8,128)} %bitcast.25), channel_id=1, replica_groups=mesh['sx'=4,'ly'=32] {'sx','ly'}, dimensions={0} | all-to-all | bytes 2097152 | tf_op jit(solution)/shard_map/all_to_all | solution.py:440
  335.4 0.1 reduce_sum.29
  335.5 0.1 broadcast_in_dim.8
  335.6 23.8 %all_to_all.45 = f32[128,2,8,128]{3,2,1,0:T(8,128)} all-to-all(f32[128,2,8,128]{3,2,1,0:T(8,128)S(1)} %broadcast_in_dim.8), channel_id=1, replica_groups=mesh['sx'=4,'ly'=32] {'sx','ly'}, dimensions={0} | all-to-all | bytes 2097152 | tf_op jit(solution)/shard_map/all_to_all | solution.py:440
  359.4 4.4 %all-to-all-start.5 = ((f32[8,5,16,160]{3,2,1,0:T(8,128)}), f32[8,5,16,160]{3,2,1,0:T(8,128)S(1)}, u32[]{:S(2)}, u32[]{:S(2)}) async-start(f32[8,5,16,160]{3,2,1,0:T(8,128)} %get-tuple-element.17), calls=%async_computation.5 | async-start | bytes 1310720 | tf_op jit(solution)/shard_map/all_to_all | solution.py:440
  363.8 9.4 %last_stage.1 = (f32[160,1280]{1,0:T(8,128)}, f32[160,256]{1,0:T(8,128)}) custom-call(f32[256,8,128]{2,1,0:T(8,128)} %bitcast.21), custom_call_target="tpu_custom_call" | custom-call | tf_op jit(solution)/shard_map/last_stage/pallas_call | solution.py:409
  373.2 1.4 all-to-all-done.5
  374.6 0.0 copy-start.1
  374.6 0.8 copy-done.1
  375.4 2.6 basis_stage.1
  (1 shorter events, 0.0 us)
Async XLA Ops:
  39.0 20.9 %all-to-all-start.1 = ((f32[128,5,2,128]{3,2,1,0:T(2,128)}), f32[128,5,2,128]{3,2,1,0:T(2,128)S(1)}, u32[]{:S(2)}, u32[]{:S(2)}) async-start(f32[128,5,2,128]{3,2,1,0:T(2,128)} %broadcast_in_dim.6), calls=%async_computation.1 | async-start | bytes 1310720 | tf_op jit(solution)/shard_map/all_to_all | solution.py:440
  59.9 0.8 copy-start
  359.4 15.2 %all-to-all-start.5 = ((f32[8,5,16,160]{3,2,1,0:T(8,128)}), f32[8,5,16,160]{3,2,1,0:T(8,128)S(1)}, u32[]{:S(2)}, u32[]{:S(2)}) async-start(f32[8,5,16,160]{3,2,1,0:T(8,128)} %get-tuple-element.17), calls=%async_computation.5 | async-start | bytes 1310720 | tf_op jit(solution)/shard_map/all_to_all | solution.py:440
  374.6 0.8 copy-start.1

commit v2 on v1

--- a/solution.py
+++ b/solution.py
@@ -11,10 +11,10 @@
 HI = lax.Precision.HIGHEST
 F32 = jnp.float32
 VMEM_LIMIT = 56 * 1024 * 1024
-UNROLL = 4
-
-
-GROUP = 5
+UNROLL = 10
+
+
+GROUP = 10
 
 
 def tiles_of(ref, size, row0=0):
@@ -50,9 +50,9 @@
                 if i == 7:
                     break
                 factor = block[i] * spread(i, 1.0 / block[i])
-                factor = jnp.where(sub > i, factor, 0.0)
                 for m in range(i + 1, 8):
                     block[m] = block[m] - factor * spread(i, block[m])
+                factor = jnp.where(sub > i, factor, 0.0)
                 for c in range(i + 1):
                     unit[c] = unit[c] - factor * spread(i, unit[c])
             root = lax.rsqrt(diag)
@@ -184,6 +184,7 @@
         dims = (((1,), (1,)), ((), ()))
         return lax.dot_general(x, y, dims, preferred_element_type=F32)
 
+    turned = fz_ref[...].T
     total = None
     for i in range(span):
         rows = pl.ds(i, rows_x, stride=span)
@@ -194,7 +195,7 @@
         part = first[:rank] + (
             (first[rank : 2 * rank] + second[:rank]) + (first[2 * rank :] + (second[rank:] + third))
         )
-        part = part * fz_ref[0, :, i : i + 1]
+        part = part * turned[:, i : i + 1]
         total = part if total is None else total + part
 
     @pl.when(step == 0)
@@ -217,7 +218,6 @@
     rank = fy_t.shape[0]
     steps = cols_z // 8
     blocks = cols_y // 128
-    fz = factor_z.reshape(steps, 8, rank).transpose(0, 2, 1)
     return pl.pallas_call(
         sketch_kernel,
         grid=(steps,),
@@ -228,7 +228,7 @@
                 for l in range(blocks)
             ),
             pl.BlockSpec((rank, cols_y), lambda i: (0, 0)),
-            pl.BlockSpec((1, rank, 8), lambda i: (i, 0, 0)),
+            pl.BlockSpec((8, rank), lambda i: (i, 0)),
         ],
         out_specs=pl.BlockSpec((rank * rows_x // 128, 128), lambda i: (0, 0)),
         scratch_shapes=[
@@ -237,7 +237,7 @@
         ],
         compiler_params=pltpu.CompilerParams(vmem_limit_bytes=VMEM_LIMIT),
         name="local_sketch",
-    )(*[tensor] * blocks, fy_t, fz)
+    )(*[tensor] * blocks, fy_t, factor_z)
 
 
 def product_kernel(qt_ref, slab_ref, out_ref, left_ref, *, cols_z, rows_x, parts, rank_part):

time: 379 us -> 375 us (0.989)
  no operation moved by 1% of the time
where the time goes in v2:
time: 375 us; the launch traced here: 374 us
  blocking collectives  254 us (68%)
  Pallas kernels  88.8 us (24%)
  waiting for transfers between devices  16.8 us (4%)
  starting transfers between devices  10.3 us (3%)
    all_to_all x6, blocking collectives, swap(): lax.all_to_all(pieces, axes, 0, 0, axis_index_groups=groups, tiled=True)  254 us
    pallas_call x1, Pallas kernels, product(): pl.pallas_call(functools.partial(product_kernel, cols_z=cols_z, rows_x=ro...  18.3 us
    pallas_call x1, Pallas kernels, local_sketch(): pl.pallas_call(sketch_kernel, grid=(steps,), out_shape=jax.ShapeDtypeStru...  18.1 us
    pallas_call x1, Pallas kernels, first_basis(): pl.pallas_call(functools.partial(first_kernel, rank=rank, scale=scale), o...  17.2 us
    all_to_all x2, waiting for transfers between devices, swap(): lax.all_to_all(pieces, axes, 0, 0, axis_index_groups=groups, tiled=True)  16.8 us
    pallas_call x1, Pallas kernels, middle_stage(): pl.pallas_call(functools.partial(middle_kernel, width=width), out_shape=(...  12.4 us
    pallas_call x1, Pallas kernels, second_stage(): pl.pallas_call(functools.partial(second_kernel, width=width), grid=(ranks...  11.1 us
    all_to_all x2, starting transfers between devices, swap(): lax.all_to_all(pieces, axes, 0, 0, axis_index_groups=groups, tiled=True)  10.3 us
  transfers between devices with their start and end apart: 2, of which 2 were waited for; matrix products, arithmetic and copies ran while one was open for 0% of the time, Pallas kernels for 2%

profile of v2, /device:TPU:1, one launch (start us, length us, event | category | flops | bytes accessed | tf_op | source)
XLA Modules:
  0.0 373.7 jit_solution(4778939339139181492)
XLA Ops:
  0.6 18.1 %local_sketch.1 = f32[320,128]{1,0:T(8,128)} custom-call(f32[256,40,512]{2,1,0:T(8,128)} %refs_3_.1, f32[256,40,512]{2,1,0:T(8,128)} %refs_3_.1, f32[256,40,512]{2,1,0:T(8,128)} %refs_3_.1, f32[256,40,512]{2,1,0:T(8,128)} %refs_3_.1, f32[160,512]{1,0:T(8,128)} %bitcast.28, f32[40,160]{1,0:T(8,128)} %refs_5_.1), custom_call_target="tpu_custom_call" | custom-call | tf_op jit(solution)/shard_map/local_sketch/pallas_call | solution.py:221
  18.8 17.3 %all_to_all.40 = f32[160,2,128]{2,1,0:T(2,128)S(1)} all-to-all(f32[160,2,128]{2,1,0:T(2,128)} %bitcast.25), channel_id=1, replica_groups=mesh['sx'=4,'ly'=32] {'ly'}, dimensions={0} | all-to-all | bytes 327680 | tf_op jit(solution)/shard_map/all_to_all | solution.py:440
  36.1 0.1 reduce_sum.27
  36.2 1.0 broadcast_in_dim.6
  37.2 5.9 %all-to-all-start.1 = ((f32[128,5,2,128]{3,2,1,0:T(2,128)}), f32[128,5,2,128]{3,2,1,0:T(2,128)S(1)}, u32[]{:S(2)}, u32[]{:S(2)}) async-start(f32[128,5,2,128]{3,2,1,0:T(2,128)} %broadcast_in_dim.6), calls=%async_computation.1 | async-start | bytes 1310720 | tf_op jit(solution)/shard_map/all_to_all | solution.py:440
  43.1 15.0 %all-to-all-done.1 = f32[128,5,2,128]{3,2,1,0:T(2,128)S(1)} async-done(((f32[128,5,2,128]{3,2,1,0:T(2,128)}), f32[128,5,2,128]{3,2,1,0:T(2,128)S(1)}, u32[]{:S(2)}, u32[]{:S(2)}) %all-to-all-start.1) | async-done | bytes 655392 | tf_op jit(solution)/shard_map/all_to_all | solution.py:440
  58.1 0.0 copy-start
  58.1 0.8 copy-done
  58.9 17.2 %first_basis.1 = (f32[160,256]{1,0:T(8,128)}, f32[160,256]{1,0:T(8,128)}) custom-call(s32[1]{0:T(128)} %bitcast.index_ref, f32[1280,128]{1,0:T(8,128)} %bitcast.20), custom_call_target="tpu_custom_call" | custom-call | tf_op jit(solution)/shard_map/first_basis/pallas_call | solution.py:156
  76.1 18.3 %product.1 = f32[4,4,1600,128]{3,2,1,0:T(8,128)} custom-call(f32[160,256]{1,0:T(8,128)} %get-tuple-element.13.qt_ref, f32[10240,512]{1,0:T(8,128)} %bitcast.16), custom_call_target="tpu_custom_call" | custom-call | tf_op jit(solution)/shard_map/product/pallas_call | solution.py:277
  94.4 154.1 %all_to_all.41 = f32[128,5,40,128]{3,2,1,0:T(8,128)} all-to-all(f32[128,5,40,128]{3,2,1,0:T(8,128)} %bitcast.18), channel_id=1, replica_groups=mesh['sx'=4,'ly'=32] {'sx','ly'}, dimensions={0} | all-to-all | bytes 26214400 | tf_op jit(solution)/shard_map/all_to_all | solution.py:440
  248.5 11.1 %second_stage.1 = (f32[1280,640]{1,0:T(8,128)}, f32[160,640]{1,0:T(8,128)}, f32[512,128]{1,0:T(8,128)}) custom-call(f32[4,32,5,40,128]{4,3,2,1,0:T(8,128)} %bitcast.17, f32[160,1280]{1,0:T(8,128)} %bitcast.24), custom_call_target="tpu_custom_call" | custom-call | tf_op jit(solution)/shard_map/second_stage/pallas_call | solution.py:323
  259.6 19.6 %all_to_all.42 = f32[128,4,128]{2,1,0:T(4,128)S(1)} all-to-all(f32[128,4,128]{2,1,0:T(4,128)} %bitcast.29), channel_id=1, replica_groups=mesh['sx'=4,'ly'=32] {'sx','ly'}, dimensions={0} | all-to-all | bytes 524288 | tf_op jit(solution)/shard_map/all_to_all | solution.py:440
  279.3 0.1 reduce_sum.28
  279.4 15.3 %all_to_all.43 = f32[128,4,128]{2,1,0:T(4,128)} all-to-all(f32[128,4,128]{2,1,0:T(4,128)S(1)} %broadcast_in_dim.7), channel_id=1, replica_groups=mesh['sx'=4,'ly'=32] {'sx','ly'}, dimensions={0} | all-to-all | bytes 524288 | tf_op jit(solution)/shard_map/all_to_all | solution.py:440
  294.7 12.4 %middle_stage.1 = (f32[8,5,16,160]{3,2,1,0:T(8,128)}, f32[256,8,128]{2,1,0:T(8,128)}) custom-call(f32[512,128]{1,0:T(8,128)} %bitcast.23, f32[160,640]{1,0:T(8,128)} %get-tuple-element.15.second_ref, f32[1280,640]{1,0:T(8,128)} %get-tuple-element.16.core_ref), custom_call_target="tpu_custom_call" | custom-call | tf_op jit(solution)/shard_map/middle_stage/pallas_call | solution.py:377
  307.2 23.9 %all_to_all.44 = f32[128,2,8,128]{3,2,1,0:T(8,128)S(1)} all-to-all(f32[128,2,8,128]{3,2,1,0:T(8,128)} %bitcast.22), channel_id=1, replica_groups=mesh['sx'=4,'ly'=32] {'sx','ly'}, dimensions={0} | all-to-all | bytes 2097152 | tf_op jit(solution)/shard_map/all_to_all | solution.py:440
  331.0 0.1 reduce_sum.29
  331.2 0.1 broadcast_in_dim.8
  331.3 23.8 %all_to_all.45 = f32[128,2,8,128]{3,2,1,0:T(8,128)} all-to-all(f32[128,2,8,128]{3,2,1,0:T(8,128)S(1)} %broadcast_in_dim.8), channel_id=1, replica_groups=mesh['sx'=4,'ly'=32] {'sx','ly'}, dimensions={0} | all-to-all | bytes 2097152 | tf_op jit(solution)/shard_map/all_to_all | solution.py:440
  355.1 4.4 %all-to-all-start.5 = ((f32[8,5,16,160]{3,2,1,0:T(8,128)}), f32[8,5,16,160]{3,2,1,0:T(8,128)S(1)}, u32[]{:S(2)}, u32[]{:S(2)}) async-start(f32[8,5,16,160]{3,2,1,0:T(8,128)} %get-tuple-element.17), calls=%async_computation.5 | async-start | bytes 1310720 | tf_op jit(solution)/shard_map/all_to_all | solution.py:440
  359.5 9.0 %last_stage.1 = (f32[160,1280]{1,0:T(8,128)}, f32[160,256]{1,0:T(8,128)}) custom-call(f32[256,8,128]{2,1,0:T(8,128)} %bitcast.19), custom_call_target="tpu_custom_call" | custom-call | tf_op jit(solution)/shard_map/last_stage/pallas_call | solution.py:409
  368.5 1.8 all-to-all-done.5
  370.2 0.0 copy-start.1
  370.2 0.8 copy-done.1
  371.1 2.6 basis_stage.1
  (1 shorter events, 0.0 us)
Async XLA Ops:
  37.2 20.9 %all-to-all-start.1 = ((f32[128,5,2,128]{3,2,1,0:T(2,128)}), f32[128,5,2,128]{3,2,1,0:T(2,128)S(1)}, u32[]{:S(2)}, u32[]{:S(2)}) async-start(f32[128,5,2,128]{3,2,1,0:T(2,128)} %broadcast_in_dim.6), calls=%async_computation.1 | async-start | bytes 1310720 | tf_op jit(solution)/shard_map/all_to_all | solution.py:440
  58.1 0.8 copy-start
  355.1 15.2 %all-to-all-start.5 = ((f32[8,5,16,160]{3,2,1,0:T(8,128)}), f32[8,5,16,160]{3,2,1,0:T(8,128)S(1)}, u32[]{:S(2)}, u32[]{:S(2)}) async-start(f32[8,5,16,160]{3,2,1,0:T(8,128)} %get-tuple-element.17), calls=%async_computation.5 | async-start | bytes 1310720 | tf_op jit(solution)/shard_map/all_to_all | solution.py:440
  370.2 0.8 copy-start.1

commit v3 on v2

--- a/solution.py
+++ b/solution.py
@@ -298,19 +298,13 @@
     core = core.reshape(core_ref.shape)
     core_ref[...] = core
     sec = dot_six(test_ref[...], core)
-    second_ref[...] = sec
-    part = dot_six(sec, sec, True)
-
-    @pl.when(step == 0)
-    def _():
-        gram_ref[:, :width] = part
-
-    @pl.when(step > 0)
-    def _():
-        gram_ref[:, :width] = gram_ref[:, :width] + part
+    lanes = core_ref.shape[1]
+    second_ref[:, pl.ds(pl.multiple_of(step * lanes, lanes), lanes)] = sec
 
     @pl.when(step == pl.num_programs(0) - 1)
     def _():
+        whole = second_ref[...]
+        gram_ref[:, :width] = dot_six(whole, whole, True)
         gram_out_ref[...] = jnp.zeros_like(gram_out_ref)
         gram_out_ref[:width, :] = gram_ref[:, :128]
         gram_out_ref[width : 2 * width, : width - 128] = gram_ref[:, 128:width]
@@ -334,7 +328,7 @@
         ],
         out_specs=(
             pl.BlockSpec((total_z, lanes), lambda i: (0, i)),
-            pl.BlockSpec((width, lanes), lambda i: (0, i)),
+            pl.BlockSpec((width, ranks * lanes), lambda i: (0, 0)),
             pl.BlockSpec((gram_rows, 128), lambda i: (0, 0)),
         ),
         scratch_shapes=[pltpu.VMEM((width, -(-width // 128) * 128), F32)],

time: 375 us -> 374 us (level)
  no operation moved by 1% of the time
where the time goes in v3:
time: 374 us; the launch traced here: 373 us
  blocking collectives  254 us (68%)
  Pallas kernels  88.3 us (24%)
  waiting for transfers between devices  16.8 us (4%)
  starting transfers between devices  10.3 us (3%)
    all_to_all x6, blocking collectives, swap(): lax.all_to_all(pieces, axes, 0, 0, axis_index_groups=groups, tiled=True)  254 us
    pallas_call x1, Pallas kernels, product(): pl.pallas_call(functools.partial(product_kernel, cols_z=cols_z, rows_x=ro...  18.3 us
    pallas_call x1, Pallas kernels, local_sketch(): pl.pallas_call(sketch_kernel, grid=(steps,), out_shape=jax.ShapeDtypeStru...  18.1 us
    pallas_call x1, Pallas kernels, first_basis(): pl.pallas_call(functools.partial(first_kernel, rank=rank, scale=scale), o...  17.2 us
    all_to_all x2, waiting for transfers between devices, swap(): lax.all_to_all(pieces, axes, 0, 0, axis_index_groups=groups, tiled=True)  16.8 us
    pallas_call x1, Pallas kernels, middle_stage(): pl.pallas_call(functools.partial(middle_kernel, width=width), out_shape=(...  12.4 us
    pallas_call x1, Pallas kernels, second_stage(): pl.pallas_call(functools.partial(second_kernel, width=width), grid=(ranks...  10.6 us
    all_to_all x2, starting transfers between devices, swap(): lax.all_to_all(pieces, axes, 0, 0, axis_index_groups=groups, tiled=True)  10.3 us
  transfers between devices with their start and end apart: 2, of which 2 were waited for; matrix products, arithmetic and copies ran while one was open for 0% of the time, Pallas kernels for 2%

profile of v3, /device:TPU:1, one launch (start us, length us, event | category | flops | bytes accessed | tf_op | source)
XLA Modules:
  0.0 373.2 jit_solution(11065769576459628718)
XLA Ops:
  0.6 18.1 %local_sketch.1 = f32[320,128]{1,0:T(8,128)} custom-call(f32[256,40,512]{2,1,0:T(8,128)} %refs_3_.1, f32[256,40,512]{2,1,0:T(8,128)} %refs_3_.1, f32[256,40,512]{2,1,0:T(8,128)} %refs_3_.1, f32[256,40,512]{2,1,0:T(8,128)} %refs_3_.1, f32[160,512]{1,0:T(8,128)} %bitcast.28, f32[40,160]{1,0:T(8,128)} %refs_5_.1), custom_call_target="tpu_custom_call" | custom-call | tf_op jit(solution)/shard_map/local_sketch/pallas_call | solution.py:221
  18.8 17.3 %all_to_all.40 = f32[160,2,128]{2,1,0:T(2,128)S(1)} all-to-all(f32[160,2,128]{2,1,0:T(2,128)} %bitcast.25), channel_id=1, replica_groups=mesh['sx'=4,'ly'=32] {'ly'}, dimensions={0} | all-to-all | bytes 327680 | tf_op jit(solution)/shard_map/all_to_all | solution.py:434
  36.1 0.1 reduce_sum.27
  36.2 1.0 broadcast_in_dim.6
  37.2 5.9 %all-to-all-start.1 = ((f32[128,5,2,128]{3,2,1,0:T(2,128)}), f32[128,5,2,128]{3,2,1,0:T(2,128)S(1)}, u32[]{:S(2)}, u32[]{:S(2)}) async-start(f32[128,5,2,128]{3,2,1,0:T(2,128)} %broadcast_in_dim.6), calls=%async_computation.1 | async-start | bytes 1310720 | tf_op jit(solution)/shard_map/all_to_all | solution.py:434
  43.1 15.0 %all-to-all-done.1 = f32[128,5,2,128]{3,2,1,0:T(2,128)S(1)} async-done(((f32[128,5,2,128]{3,2,1,0:T(2,128)}), f32[128,5,2,128]{3,2,1,0:T(2,128)S(1)}, u32[]{:S(2)}, u32[]{:S(2)}) %all-to-all-start.1) | async-done | bytes 655392 | tf_op jit(solution)/shard_map/all_to_all | solution.py:434
  58.1 0.0 copy-start
  58.1 0.8 copy-done
  58.9 17.2 %first_basis.1 = (f32[160,256]{1,0:T(8,128)}, f32[160,256]{1,0:T(8,128)}) custom-call(s32[1]{0:T(128)} %bitcast.index_ref, f32[1280,128]{1,0:T(8,128)} %bitcast.20), custom_call_target="tpu_custom_call" | custom-call | tf_op jit(solution)/shard_map/first_basis/pallas_call | solution.py:156
  76.1 18.3 %product.1 = f32[4,4,1600,128]{3,2,1,0:T(8,128)} custom-call(f32[160,256]{1,0:T(8,128)} %get-tuple-element.13.qt_ref, f32[10240,512]{1,0:T(8,128)} %bitcast.16), custom_call_target="tpu_custom_call" | custom-call | tf_op jit(solution)/shard_map/product/pallas_call | solution.py:277
  94.4 154.1 %all_to_all.41 = f32[128,5,40,128]{3,2,1,0:T(8,128)} all-to-all(f32[128,5,40,128]{3,2,1,0:T(8,128)} %bitcast.18), channel_id=1, replica_groups=mesh['sx'=4,'ly'=32] {'sx','ly'}, dimensions={0} | all-to-all | bytes 26214400 | tf_op jit(solution)/shard_map/all_to_all | solution.py:434
  248.5 10.6 %second_stage.1 = (f32[1280,640]{1,0:T(8,128)}, f32[160,640]{1,0:T(8,128)}, f32[512,128]{1,0:T(8,128)}) custom-call(f32[4,32,5,40,128]{4,3,2,1,0:T(8,128)} %bitcast.17, f32[160,1280]{1,0:T(8,128)} %bitcast.24), custom_call_target="tpu_custom_call" | custom-call | tf_op jit(solution)/shard_map/second_stage/pallas_call | solution.py:317
  259.2 19.6 %all_to_all.42 = f32[128,4,128]{2,1,0:T(4,128)S(1)} all-to-all(f32[128,4,128]{2,1,0:T(4,128)} %bitcast.29), channel_id=1, replica_groups=mesh['sx'=4,'ly'=32] {'sx','ly'}, dimensions={0} | all-to-all | bytes 524288 | tf_op jit(solution)/shard_map/all_to_all | solution.py:434
  278.8 0.1 reduce_sum.28
  279.0 15.3 %all_to_all.43 = f32[128,4,128]{2,1,0:T(4,128)} all-to-all(f32[128,4,128]{2,1,0:T(4,128)S(1)} %broadcast_in_dim.7), channel_id=1, replica_groups=mesh['sx'=4,'ly'=32] {'sx','ly'}, dimensions={0} | all-to-all | bytes 524288 | tf_op jit(solution)/shard_map/all_to_all | solution.py:434
  294.2 12.4 %middle_stage.1 = (f32[8,5,16,160]{3,2,1,0:T(8,128)}, f32[256,8,128]{2,1,0:T(8,128)}) custom-call(f32[512,128]{1,0:T(8,128)} %bitcast.23, f32[160,640]{1,0:T(8,128)} %get-tuple-element.15.second_ref, f32[1280,640]{1,0:T(8,128)} %get-tuple-element.16.core_ref), custom_call_target="tpu_custom_call" | custom-call | tf_op jit(solution)/shard_map/middle_stage/pallas_call | solution.py:371
  306.7 23.9 %all_to_all.44 = f32[128,2,8,128]{3,2,1,0:T(8,128)S(1)} all-to-all(f32[128,2,8,128]{3,2,1,0:T(8,128)} %bitcast.22), channel_id=1, replica_groups=mesh['sx'=4,'ly'=32] {'sx','ly'}, dimensions={0} | all-to-all | bytes 2097152 | tf_op jit(solution)/shard_map/all_to_all | solution.py:434
  330.6 0.1 reduce_sum.29
  330.7 0.1 broadcast_in_dim.8
  330.8 23.8 %all_to_all.45 = f32[128,2,8,128]{3,2,1,0:T(8,128)} all-to-all(f32[128,2,8,128]{3,2,1,0:T(8,128)S(1)} %broadcast_in_dim.8), channel_id=1, replica_groups=mesh['sx'=4,'ly'=32] {'sx','ly'}, dimensions={0} | all-to-all | bytes 2097152 | tf_op jit(solution)/shard_map/all_to_all | solution.py:434
  354.6 4.4 %all-to-all-start.5 = ((f32[8,5,16,160]{3,2,1,0:T(8,128)}), f32[8,5,16,160]{3,2,1,0:T(8,128)S(1)}, u32[]{:S(2)}, u32[]{:S(2)}) async-start(f32[8,5,16,160]{3,2,1,0:T(8,128)} %get-tuple-element.17), calls=%async_computation.5 | async-start | bytes 1310720 | tf_op jit(solution)/shard_map/all_to_all | solution.py:434
  359.0 9.0 %last_stage.1 = (f32[160,1280]{1,0:T(8,128)}, f32[160,256]{1,0:T(8,128)}) custom-call(f32[256,8,128]{2,1,0:T(8,128)} %bitcast.19), custom_call_target="tpu_custom_call" | custom-call | tf_op jit(solution)/shard_map/last_stage/pallas_call | solution.py:403
  368.0 1.8 all-to-all-done.5
  369.8 0.0 copy-start.1
  369.8 0.8 copy-done.1
  370.6 2.6 basis_stage.1
  (1 shorter events, 0.0 us)
Async XLA Ops:
  37.2 20.9 %all-to-all-start.1 = ((f32[128,5,2,128]{3,2,1,0:T(2,128)}), f32[128,5,2,128]{3,2,1,0:T(2,128)S(1)}, u32[]{:S(2)}, u32[]{:S(2)}) async-start(f32[128,5,2,128]{3,2,1,0:T(2,128)} %broadcast_in_dim.6), calls=%async_computation.1 | async-start | bytes 1310720 | tf_op jit(solution)/shard_map/all_to_all | solution.py:434
  58.1 0.8 copy-start
  354.6 15.2 %all-to-all-start.5 = ((f32[8,5,16,160]{3,2,1,0:T(8,128)}), f32[8,5,16,160]{3,2,1,0:T(8,128)S(1)}, u32[]{:S(2)}, u32[]{:S(2)}) async-start(f32[8,5,16,160]{3,2,1,0:T(8,128)} %get-tuple-element.17), calls=%async_computation.5 | async-start | bytes 1310720 | tf_op jit(solution)/shard_map/all_to_all | solution.py:434
  369.8 0.8 copy-start.1
